TPU v7x, 32 devices: a whole 2x2x4 slice. The times are simulated.
32 devices in a mesh: row: 4 (over y, x), col: 8 (over z, core).
Axes of the slice: x: 2, y: 2, z: 4, core: 2. Of those that a mesh axis runs over, the one named last changes fastest.
Arguments:
- operators: float32 [4, 8, 768, 768], P('row', 'col'), may hold values from -0.1875 to 0.1875
- positions: int32 [4, 8, 256], P('row', 'col'), may hold values from 0 to 767
- amplitudes: float32 [4, 8, 256], P('row', 'col'), may hold values from -96 to 96
Outputs:
- traces: float32 [4, 8, 256, 768], P('row', 'col')
All inputs are finite; a program needn't handle non-finite values.
Results may differ from a plain program's by a relative error of at most 0.0003.
Values sent between devices are 32-bit elements; how exact they have to be, the bound alone decides.
A program may use at most 64 MiB of HBM per device.

v0:
```python
import functools

import jax
import jax.numpy as jnp
from jax import lax
from jax.experimental import pallas as pl
from jax.experimental.pallas import tpu as pltpu
from jax.sharding import PartitionSpec as P

BATCH = 32
CORE_HOP, CHIP_HOP, ROW_HOP, FAR_HOP, PERIOD = 16, 26, 28, 36, 1
MESH = pl.DeviceIdType.MESH


def kernel(
    rows, cols, op_hbm, pos_ref, amp_ref, out_ref,
    op_f32, hi_ref, lo_ref, hi_turned, lo_turned, pos_all, amp_all,
    north_in, west_in, south_in, east_in,
    south_out, east_out, north_out, west_out,
    op_sem, send_sem, recv_sem,
):
    row = lax.axis_index("row")
    col = lax.axis_index("col")
    batches, batch, half = north_in.shape
    order = 2 * half
    has_north, has_south = row > 0, row < rows - 1
    has_west, has_east = col > 0, col < cols - 1

    load = pltpu.make_async_copy(op_hbm.at[0, 0], op_f32, op_sem)
    load.start()

    barrier = pltpu.get_barrier_semaphore()
    sides = (
        (has_north, (row - 1, col)),
        (has_south, (row + 1, col)),
        (has_west, (row, col - 1)),
        (has_east, (row, col + 1)),
    )
    count = 0
    for present, where in sides:
        count = count + present.astype(jnp.int32)

        @pl.when(present)
        def _(where=where):
            pl.semaphore_signal(barrier, inc=1, device_id=where, device_id_type=MESH)

    for present, ref in ((has_north, north_in), (has_west, west_in), (has_south, south_in), (has_east, east_in)):
        @pl.when(jnp.logical_not(present))
        def _(ref=ref):
            ref[...] = jnp.zeros_like(ref)

    shots = batches * batch
    pos_all[...] = jnp.transpose(jnp.broadcast_to(pos_ref[0], (128, shots)))
    amp_all[...] = jnp.transpose(jnp.broadcast_to(amp_ref[0], (128, shots)))

    def split(value, high_ref, low_ref):
        high = value.astype(jnp.bfloat16)
        high_ref[...] = high
        low_ref[...] = (value - high.astype(jnp.float32)).astype(jnp.bfloat16)

    pl.semaphore_wait(barrier, count)

    def link(kind, b):
        src, dst, where = (
            (south_out, north_in, (row + 1, col)),
            (east_out, west_in, (row, col + 1)),
            (north_out, south_in, (row - 1, col)),
            (west_out, east_in, (row, col - 1)),
        )[kind]
        return pltpu.make_async_remote_copy(
            src_ref=src.at[b], dst_ref=dst.at[b],
            send_sem=send_sem.at[kind, b], recv_sem=recv_sem.at[kind, b],
            device_id=where, device_id_type=MESH,
        )

    def product(both, high, adjoint):
        wide, narrow = (hi_turned, lo_turned) if adjoint else (hi_ref, lo_ref)
        first = jnp.dot(both, wide[...], preferred_element_type=jnp.float32)
        second = jnp.dot(high, narrow[...], preferred_element_type=jnp.float32)
        return first[:batch] + (first[batch:] + second)

    def source(b, width, offset):
        at = pl.ds(pl.multiple_of(b * batch, batch), batch)
        spot, strength = pos_all[at, :], amp_all[at, :]
        lanes = lax.broadcasted_iota(jnp.int32, (batch, 128), 1)
        return jnp.concatenate(
            [jnp.where(lanes + (offset + j) == spot, strength, 0.0) for j in range(0, width, 128)], axis=1
        )

    def corner(b, row_out, col_out, put_row, put_col, row_kind, col_kind):
        row_out[b] = source(b, half, 0)
        col_out[b] = source(b, half, half)

        @pl.when(put_row)
        def _():
            link(row_kind, b).start()

        @pl.when(put_col)
        def _():
            link(col_kind, b).start()

    def cell(b, adjoint, row_in, col_in, got_row, got_col, row_out, col_out, put_row, put_col, row_kind, col_kind):
        @pl.when(got_row)
        def _():
            link(row_kind, b).wait_recv()

        @pl.when(got_col)
        def _():
            link(col_kind, b).wait_recv()

        inputs = jnp.concatenate([row_in[b], col_in[b]], axis=1)
        high = inputs.astype(jnp.bfloat16)
        low = (inputs - high.astype(jnp.float32)).astype(jnp.bfloat16)
        both = jnp.concatenate([high, low], axis=0)
        result = product(both, high, adjoint) + source(b, order, 0)
        row_out[b] = result[:, :half]

        @pl.when(put_row)
        def _():
            link(row_kind, b).start()

        col_out[b] = result[:, half:]

        @pl.when(put_col)
        def _():
            link(col_kind, b).start()

    def reach(r, c):
        return (r * ROW_HOP + (r // 2) * (FAR_HOP - ROW_HOP)
                + ((c + 1) // 2) * CORE_HOP + (c // 2) * CHIP_HOP)

    lead_fwd = reach(row, col)
    lead_adj = reach(rows - 1, cols - 1) - lead_fwd
    first_cell = jnp.logical_not(jnp.logical_or(has_north, has_west))
    last_cell = jnp.logical_not(jnp.logical_or(has_south, has_east))

    @pl.when(first_cell)
    def _():
        lax.fori_loop(0, batches, lambda b, carry: (corner(
            b, south_out, east_out, has_south, has_east, 0, 1), carry)[1], 0)

    @pl.when(last_cell)
    def _():
        lax.fori_loop(0, batches, lambda b, carry: (corner(
            b, north_out, west_out, has_north, has_west, 2, 3), carry)[1], 0)

    load.wait()
    split(op_f32[...], hi_ref, lo_ref)
    turn_at = jnp.where(row + col == 1, batches, 0)

    def tick(step, carry):
        fwd, adj = carry
        fwd_next = jnp.logical_and(
            fwd < batches,
            jnp.logical_or(adj >= batches, lead_fwd + fwd * PERIOD <= lead_adj + adj * PERIOD),
        )

        @pl.when(step == turn_at)
        def _():
            split(jnp.transpose(op_f32[...]), hi_turned, lo_turned)

        @pl.when(jnp.logical_and(fwd_next, jnp.logical_not(first_cell)))
        def _():
            cell(fwd, False, north_in, west_in, has_north, has_west,
                 south_out, east_out, has_south, has_east, 0, 1)

        @pl.when(jnp.logical_not(jnp.logical_or(fwd_next, last_cell)))
        def _():
            cell(adj, True, south_in, east_in, has_south, has_east,
                 north_out, west_out, has_north, has_west, 2, 3)

        done = jnp.where(fwd_next, fwd, adj)

        @pl.when(jnp.where(fwd_next, fwd < adj, adj < fwd))
        def _():
            at = pl.ds(pl.multiple_of(done * batch, batch), batch)
            out_ref[0, 0, at, :half] = south_out[done] + north_out[done]
            out_ref[0, 0, at, half:] = east_out[done] + west_out[done]

        moved = fwd_next.astype(jnp.int32)
        return fwd + moved, adj + 1 - moved

    lax.fori_loop(0, 2 * batches, tick, (jnp.int32(0), jnp.int32(0)))

    def drain(b, carry):
        for kind, present in enumerate((has_south, has_east, has_north, has_west)):
            @pl.when(present)
            def _(kind=kind):
                link(kind, b).wait_send()
        return carry

    lax.fori_loop(0, batches, drain, 0)


def local(rows, cols, operators, positions, amplitudes):
    order = operators.shape[-1]
    shots = positions.shape[-1]
    half = order // 2
    batches = shots // BATCH
    slots = pltpu.VMEM((batches, BATCH, half), jnp.float32)
    return pl.pallas_call(
        functools.partial(kernel, rows, cols),
        out_shape=jax.ShapeDtypeStruct((1, 1, shots, order), jnp.float32),
        in_specs=[
            pl.BlockSpec(memory_space=pltpu.HBM),
            pl.BlockSpec(memory_space=pltpu.VMEM),
            pl.BlockSpec(memory_space=pltpu.VMEM),
        ],
        out_specs=pl.BlockSpec(memory_space=pltpu.VMEM),
        scratch_shapes=[
            pltpu.VMEM((order, order), jnp.float32),
            pltpu.VMEM((order, order), jnp.bfloat16),
            pltpu.VMEM((order, order), jnp.bfloat16),
            pltpu.VMEM((order, order), jnp.bfloat16),
            pltpu.VMEM((order, order), jnp.bfloat16),
            pltpu.VMEM((shots, 128), jnp.int32),
            pltpu.VMEM((shots, 128), jnp.float32),
            slots, slots, slots, slots,
            slots, slots, slots, slots,
            pltpu.SemaphoreType.DMA,
            pltpu.SemaphoreType.DMA((4, batches)),
            pltpu.SemaphoreType.DMA((4, batches)),
        ],
        compiler_params=pltpu.CompilerParams(collective_id=0, has_side_effects=True, vmem_limit_bytes=62 << 20),
    )(operators, positions, amplitudes)


def solution(mesh):
    in_specs = (P("row", "col", None, None), P("row", "col", None), P("row", "col", None))
    out_specs = P("row", "col", None, None)
    body = functools.partial(local, mesh.shape["row"], mesh.shape["col"])
    return jax.shard_map(body, mesh=mesh, in_specs=in_specs, out_specs=out_specs, check_vma=False)
```

profile of v0, /device:TPU:0, one launch (start us, length us, event | category | flops | bytes accessed | tf_op | source)
XLA Modules:
  0.0 49.8 jit_solution(632540866323923934)
XLA Ops:
  0.0 47.7 %shard_map.37 = f32[1,1,256,768]{3,2,1,0:T(8,128)} custom-call(f32[1,1,768,768]{3,2,1,0:T(8,128)} %op_hbm.1, s32[1,1,256]{2,1,0:T(1,128)} %pos_ref.1, f32[1,1,256]{2,1,0:T(1,128)} %amp_ref.1), custom_call_target="tpu_custom_call" | custom-call | tf_op jit(solution)/shard_map/pallas_call | solution.py:201
  47.7 2.1 %copy.5 = f32[1,1,256,768]{3,2,1,0:T(8,128)} copy(f32[1,1,256,768]{3,2,1,0:T(8,128)} %shard_map.37) | data formatting | bytes 1572864
where the time goes:
time: 49.9 us; the launch traced here: 49.8 us
  Pallas kernels  47.7 us (96%)
  local copies, waits for them, and re-layouts  2.06 us (4%)
    pallas_call x1, Pallas kernels, local(): pl.pallas_call(functools.partial(kernel, rows, cols), out_shape=jax.Shape...  47.7 us
    unnamed x1, local copies, waits for them, and re-layouts  2.06 us

commit v1 on v0

--- a/solution.py
+++ b/solution.py
@@ -221,7 +221,7 @@
             pltpu.SemaphoreType.DMA((4, batches)),
             pltpu.SemaphoreType.DMA((4, batches)),
         ],
-        compiler_params=pltpu.CompilerParams(collective_id=0, has_side_effects=True, vmem_limit_bytes=62 << 20),
+        compiler_params=pltpu.CompilerParams(collective_id=0, has_side_effects=True, vmem_limit_bytes=52 << 20),
     )(operators, positions, amplitudes)
 
 

time: 49.9 us -> 48.5 us (0.972)
  Pallas kernels: 47.7 us -> 46.1 us
    pallas_call x1, Pallas kernels: 47.7 us -> 46.1 us  [local(): pl.pallas_call(functools.partial(kernel, rows, cols), out_shape=jax.Shape...]
    unnamed x1 -> x5, local copies, waits for them, and re-layouts: 2.06 us -> 2.24 us
where the time goes in v1:
time: 48.5 us; the launch traced here: 48.4 us
  Pallas kernels  46.1 us (95%)
  local copies, waits for them, and re-layouts  2.24 us (5%)
    pallas_call x1, Pallas kernels, local(): pl.pallas_call(functools.partial(kernel, rows, cols), out_shape=jax.Shape...  46.1 us
    unnamed x5, local copies, waits for them, and re-layouts  2.24 us

profile of v1, /device:TPU:0, one launch (start us, length us, event | category | flops | bytes accessed | tf_op | source)
XLA Modules:
  0.0 48.4 jit_solution(10566363258810838465)
XLA Ops:
  0.0 0.0 copy-start
  0.0 0.7 %copy-done = s32[1,1,256]{2,1,0:T(1,128)S(1)} copy-done((s32[1,1,256]{2,1,0:T(1,128)S(1)}, s32[1,1,256]{2,1,0:T(1,128)}, u32[]{:S(2)}) %copy-start) | copy-done | bytes 1048
  0.7 0.0 copy-start.1
  0.7 0.7 %copy-done.1 = f32[1,1,256]{2,1,0:T(1,128)S(1)} copy-done((f32[1,1,256]{2,1,0:T(1,128)S(1)}, f32[1,1,256]{2,1,0:T(1,128)}, u32[]{:S(2)}) %copy-start.1) | copy-done | bytes 1048
  1.4 46.1 %shard_map.37 = f32[1,1,256,768]{3,2,1,0:T(8,128)S(1)} custom-call(f32[1,1,768,768]{3,2,1,0:T(8,128)} %op_hbm.1, s32[1,1,256]{2,1,0:T(1,128)S(1)} %copy-done, f32[1,1,256]{2,1,0:T(1,128)S(1)} %copy-done.1), custom_call_target="tpu_custom_call" | custom-call | tf_op jit(solution)/shard_map/pallas_call | solution.py:201
  47.5 0.9 %copy.5 = f32[1,1,256,768]{3,2,1,0:T(8,128)} copy(f32[1,1,256,768]{3,2,1,0:T(8,128)S(1)} %shard_map.37) | data formatting | bytes 1572864
Async XLA Ops:
  0.0 0.7 %copy-start = (s32[1,1,256]{2,1,0:T(1,128)S(1)}, s32[1,1,256]{2,1,0:T(1,128)}, u32[]{:S(2)}) copy-start(s32[1,1,256]{2,1,0:T(1,128)} %pos_ref.1) | copy-start | bytes 3076
  0.7 0.7 %copy-start.1 = (f32[1,1,256]{2,1,0:T(1,128)S(1)}, f32[1,1,256]{2,1,0:T(1,128)}, u32[]{:S(2)}) copy-start(f32[1,1,256]{2,1,0:T(1,128)} %amp_ref.1) | copy-start | bytes 3076

commit v2 on v1

--- a/solution.py
+++ b/solution.py
@@ -8,7 +8,7 @@
 from jax.sharding import PartitionSpec as P
 
 BATCH = 32
-CORE_HOP, CHIP_HOP, ROW_HOP, FAR_HOP, PERIOD = 16, 26, 28, 36, 1
+CORE_HOP, CHIP_HOP, ROW_HOP, FAR_HOP, RELAY_HOP, PERIOD = 15, 32, 36, 50, 27, 5
 MESH = pl.DeviceIdType.MESH
 
 
@@ -16,8 +16,8 @@
     rows, cols, op_hbm, pos_ref, amp_ref, out_ref,
     op_f32, hi_ref, lo_ref, hi_turned, lo_turned, pos_all, amp_all,
     north_in, west_in, south_in, east_in,
-    south_out, east_out, north_out, west_out,
-    op_sem, send_sem, recv_sem,
+    south_out, east_out, north_out, west_out, passing,
+    op_sem, send_sem, recv_sem, pass_sem, onward_sem,
 ):
     row = lax.axis_index("row")
     col = lax.axis_index("col")
@@ -29,12 +29,27 @@
     load = pltpu.make_async_copy(op_hbm.at[0, 0], op_f32, op_sem)
     load.start()
 
+    middle, chip = rows // 2, cols // 4
+    partner = col + 1 - 2 * (col % 2)
+    fwd_zone, adj_zone = col // 2 == chip, col // 2 == chip - 1
+    zone = jnp.logical_or(fwd_zone, adj_zone)
+    relay_row = jnp.where(fwd_zone, rows - 1, 0)
+    from_row = jnp.where(fwd_zone, middle - 1, middle)
+    to_row = jnp.where(fwd_zone, middle, middle - 1)
+    detour = jnp.logical_and(zone, row == from_row)
+    detour_end = jnp.logical_and(zone, row == to_row)
+    relays = jnp.logical_and(zone, row == relay_row)
+
     barrier = pltpu.get_barrier_semaphore()
     sides = (
         (has_north, (row - 1, col)),
         (has_south, (row + 1, col)),
         (has_west, (row, col - 1)),
         (has_east, (row, col + 1)),
+        (detour, (relay_row, partner)),
+        (detour_end, (relay_row, partner)),
+        (relays, (from_row, partner)),
+        (relays, (to_row, partner)),
     )
     count = 0
     for present, where in sides:
@@ -57,8 +72,6 @@
         high = value.astype(jnp.bfloat16)
         high_ref[...] = high
         low_ref[...] = (value - high.astype(jnp.float32)).astype(jnp.bfloat16)
-
-    pl.semaphore_wait(barrier, count)
 
     def link(kind, b):
         src, dst, where = (
@@ -73,6 +86,44 @@
             device_id=where, device_id_type=MESH,
         )
 
+    def leave(kind, b):
+        return pltpu.make_async_remote_copy(
+            src_ref=(south_out, None, north_out)[kind].at[b], dst_ref=passing.at[b],
+            send_sem=send_sem.at[kind, b], recv_sem=pass_sem.at[b],
+            device_id=(relay_row, partner), device_id_type=MESH,
+        )
+
+    def onward(kind, b):
+        return pltpu.make_async_remote_copy(
+            src_ref=passing.at[b], dst_ref=(north_in, None, south_in)[kind].at[b],
+            send_sem=onward_sem.at[b], recv_sem=recv_sem.at[kind, b],
+            device_id=(to_row, partner), device_id_type=MESH,
+        )
+
+    def put(kind, b, present):
+        if kind % 2:
+            @pl.when(present)
+            def _():
+                link(kind, b).start()
+            return
+
+        around = jnp.logical_and(detour, (adj_zone if kind else fwd_zone))
+
+        @pl.when(jnp.logical_and(present, jnp.logical_not(around)))
+        def _():
+            link(kind, b).start()
+
+        @pl.when(around)
+        def _():
+            leave(kind, b).start()
+
+    def relay(b):
+        for kind, here in ((0, fwd_zone), (2, adj_zone)):
+            @pl.when(here)
+            def _(kind=kind):
+                leave(kind, b).wait_recv()
+                onward(kind, b).start()
+
     def product(both, high, adjoint):
         wide, narrow = (hi_turned, lo_turned) if adjoint else (hi_ref, lo_ref)
         first = jnp.dot(both, wide[...], preferred_element_type=jnp.float32)
@@ -87,17 +138,12 @@
             [jnp.where(lanes + (offset + j) == spot, strength, 0.0) for j in range(0, width, 128)], axis=1
         )
 
-    def corner(b, row_out, col_out, put_row, put_col, row_kind, col_kind):
+    def corner_cell(b, row_out, col_out, put_row, put_col, row_kind, col_kind):
         row_out[b] = source(b, half, 0)
         col_out[b] = source(b, half, half)
 
-        @pl.when(put_row)
-        def _():
-            link(row_kind, b).start()
-
-        @pl.when(put_col)
-        def _():
-            link(col_kind, b).start()
+        put(row_kind, b, put_row)
+        put(col_kind, b, put_col)
 
     def cell(b, adjoint, row_in, col_in, got_row, got_col, row_out, col_out, put_row, put_col, row_kind, col_kind):
         @pl.when(got_row)
@@ -115,78 +161,111 @@
         result = product(both, high, adjoint) + source(b, order, 0)
         row_out[b] = result[:, :half]
 
-        @pl.when(put_row)
-        def _():
-            link(row_kind, b).start()
+        put(row_kind, b, put_row)
 
         col_out[b] = result[:, half:]
 
-        @pl.when(put_col)
-        def _():
-            link(col_kind, b).start()
+        put(col_kind, b, put_col)
 
     def reach(r, c):
         return (r * ROW_HOP + (r // 2) * (FAR_HOP - ROW_HOP)
                 + ((c + 1) // 2) * CORE_HOP + (c // 2) * CHIP_HOP)
 
+    far_end = reach(rows - 1, cols - 1)
     lead_fwd = reach(row, col)
-    lead_adj = reach(rows - 1, cols - 1) - lead_fwd
+    lead_adj = far_end - lead_fwd
+    lead_pass = RELAY_HOP + jnp.where(fwd_zone, reach(from_row, partner), far_end - reach(from_row, partner))
     first_cell = jnp.logical_not(jnp.logical_or(has_north, has_west))
     last_cell = jnp.logical_not(jnp.logical_or(has_south, has_east))
 
+    corner = jnp.logical_or(first_cell, last_cell)
+
+    @pl.when(corner)
+    def _():
+        pl.semaphore_wait(barrier, count)
+
     @pl.when(first_cell)
     def _():
-        lax.fori_loop(0, batches, lambda b, carry: (corner(
+        lax.fori_loop(0, batches, lambda b, carry: (corner_cell(
             b, south_out, east_out, has_south, has_east, 0, 1), carry)[1], 0)
 
     @pl.when(last_cell)
     def _():
-        lax.fori_loop(0, batches, lambda b, carry: (corner(
+        lax.fori_loop(0, batches, lambda b, carry: (corner_cell(
             b, north_out, west_out, has_north, has_west, 2, 3), carry)[1], 0)
 
+    near_first, near_last = row + col == 1, row + col == rows + cols - 3
+    adj_first = lead_adj < lead_fwd
+
+    def plain():
+        split(op_f32[...], hi_ref, lo_ref)
+
+    def turn():
+        split(jnp.transpose(op_f32[...]), hi_turned, lo_turned)
+
     load.wait()
-    split(op_f32[...], hi_ref, lo_ref)
-    turn_at = jnp.where(row + col == 1, batches, 0)
+    pl.when(adj_first)(turn)
+    pl.when(jnp.logical_not(near_last))(plain)
+    pl.when(jnp.logical_not(jnp.logical_or(adj_first, near_first)))(turn)
+
+    @pl.when(jnp.logical_not(corner))
+    def _():
+        pl.semaphore_wait(barrier, count)
 
     def tick(step, carry):
-        fwd, adj = carry
+        fwd, adj, passed = carry
         fwd_next = jnp.logical_and(
             fwd < batches,
             jnp.logical_or(adj >= batches, lead_fwd + fwd * PERIOD <= lead_adj + adj * PERIOD),
         )
-
-        @pl.when(step == turn_at)
-        def _():
-            split(jnp.transpose(op_f32[...]), hi_turned, lo_turned)
-
-        @pl.when(jnp.logical_and(fwd_next, jnp.logical_not(first_cell)))
+        now = jnp.where(fwd_next, lead_fwd + fwd * PERIOD, lead_adj + adj * PERIOD)
+        pass_next = jnp.logical_and(
+            passed < batches,
+            jnp.logical_or(fwd + adj >= 2 * batches, lead_pass + passed * PERIOD <= now),
+        )
+        fwd_now = jnp.logical_and(fwd_next, jnp.logical_not(pass_next))
+        adj_now = jnp.logical_not(jnp.logical_or(fwd_next, pass_next))
+
+        pl.when(jnp.logical_and(near_first, step == batches))(turn)
+        pl.when(jnp.logical_and(near_last, step == batches))(plain)
+
+        @pl.when(pass_next)
+        def _():
+            relay(passed)
+
+        @pl.when(jnp.logical_and(fwd_now, jnp.logical_not(first_cell)))
         def _():
             cell(fwd, False, north_in, west_in, has_north, has_west,
                  south_out, east_out, has_south, has_east, 0, 1)
 
-        @pl.when(jnp.logical_not(jnp.logical_or(fwd_next, last_cell)))
+        @pl.when(jnp.logical_and(adj_now, jnp.logical_not(last_cell)))
         def _():
             cell(adj, True, south_in, east_in, has_south, has_east,
                  north_out, west_out, has_north, has_west, 2, 3)
 
         done = jnp.where(fwd_next, fwd, adj)
 
-        @pl.when(jnp.where(fwd_next, fwd < adj, adj < fwd))
+        @pl.when(jnp.logical_or(jnp.logical_and(fwd_now, fwd < adj), jnp.logical_and(adj_now, adj < fwd)))
         def _():
             at = pl.ds(pl.multiple_of(done * batch, batch), batch)
             out_ref[0, 0, at, :half] = south_out[done] + north_out[done]
             out_ref[0, 0, at, half:] = east_out[done] + west_out[done]
 
-        moved = fwd_next.astype(jnp.int32)
-        return fwd + moved, adj + 1 - moved
-
-    lax.fori_loop(0, 2 * batches, tick, (jnp.int32(0), jnp.int32(0)))
+        return fwd + fwd_now.astype(jnp.int32), adj + adj_now.astype(jnp.int32), passed + pass_next.astype(jnp.int32)
+
+    start_pass = jnp.where(relays, 0, batches)
+    lax.fori_loop(0, 3 * batches - start_pass, tick, (jnp.int32(0), jnp.int32(0), start_pass))
 
     def drain(b, carry):
         for kind, present in enumerate((has_south, has_east, has_north, has_west)):
             @pl.when(present)
             def _(kind=kind):
                 link(kind, b).wait_send()
+
+        @pl.when(relays)
+        def _():
+            onward(0, b).wait_send()
+
         return carry
 
     lax.fori_loop(0, batches, drain, 0)
@@ -216,10 +295,12 @@
             pltpu.VMEM((shots, 128), jnp.int32),
             pltpu.VMEM((shots, 128), jnp.float32),
             slots, slots, slots, slots,
-            slots, slots, slots, slots,
+            slots, slots, slots, slots, slots,
             pltpu.SemaphoreType.DMA,
             pltpu.SemaphoreType.DMA((4, batches)),
             pltpu.SemaphoreType.DMA((4, batches)),
+            pltpu.SemaphoreType.DMA((batches,)),
+            pltpu.SemaphoreType.DMA((batches,)),
         ],
         compiler_params=pltpu.CompilerParams(collective_id=0, has_side_effects=True, vmem_limit_bytes=52 << 20),
     )(operators, positions, amplitudes)

time: 48.5 us -> 47.1 us (0.971)
  Pallas kernels: 46.1 us -> 44.7 us
    pallas_call x1, Pallas kernels: 46.1 us -> 44.7 us  [local(): pl.pallas_call(functools.partial(kernel, rows, cols), out_shape=jax.Shape...]
where the time goes in v2:
time: 47.1 us; the launch traced here: 47 us
  Pallas kernels  44.7 us (95%)
  local copies, waits for them, and re-layouts  2.24 us (5%)
    pallas_call x1, Pallas kernels, local(): pl.pallas_call(functools.partial(kernel, rows, cols), out_shape=jax.Shape...  44.7 us
    unnamed x5, local copies, waits for them, and re-layouts  2.24 us

profile of v2, /device:TPU:0, one launch (start us, length us, event | category | flops | bytes accessed | tf_op | source)
XLA Modules:
  0.0 47.0 jit_solution(14601635976270393213)
XLA Ops:
  0.0 0.0 copy-start
  0.0 0.7 %copy-done = s32[1,1,256]{2,1,0:T(1,128)S(1)} copy-done((s32[1,1,256]{2,1,0:T(1,128)S(1)}, s32[1,1,256]{2,1,0:T(1,128)}, u32[]{:S(2)}) %copy-start) | copy-done | bytes 1048
  0.7 0.0 copy-start.1
  0.7 0.7 %copy-done.1 = f32[1,1,256]{2,1,0:T(1,128)S(1)} copy-done((f32[1,1,256]{2,1,0:T(1,128)S(1)}, f32[1,1,256]{2,1,0:T(1,128)}, u32[]{:S(2)}) %copy-start.1) | copy-done | bytes 1048
  1.4 44.7 %shard_map.37 = f32[1,1,256,768]{3,2,1,0:T(8,128)S(1)} custom-call(f32[1,1,768,768]{3,2,1,0:T(8,128)} %op_hbm.1, s32[1,1,256]{2,1,0:T(1,128)S(1)} %copy-done, f32[1,1,256]{2,1,0:T(1,128)S(1)} %copy-done.1), custom_call_target="tpu_custom_call" | custom-call | tf_op jit(solution)/shard_map/pallas_call | solution.py:280
  46.1 0.9 %copy.5 = f32[1,1,256,768]{3,2,1,0:T(8,128)} copy(f32[1,1,256,768]{3,2,1,0:T(8,128)S(1)} %shard_map.37) | data formatting | bytes 1572864
Async XLA Ops:
  0.0 0.7 %copy-start = (s32[1,1,256]{2,1,0:T(1,128)S(1)}, s32[1,1,256]{2,1,0:T(1,128)}, u32[]{:S(2)}) copy-start(s32[1,1,256]{2,1,0:T(1,128)} %pos_ref.1) | copy-start | bytes 3076
  0.7 0.7 %copy-start.1 = (f32[1,1,256]{2,1,0:T(1,128)S(1)}, f32[1,1,256]{2,1,0:T(1,128)}, u32[]{:S(2)}) copy-start(f32[1,1,256]{2,1,0:T(1,128)} %amp_ref.1) | copy-start | bytes 3076

commit v3 on v2

--- a/solution.py
+++ b/solution.py
@@ -8,16 +8,16 @@
 from jax.sharding import PartitionSpec as P
 
 BATCH = 32
-CORE_HOP, CHIP_HOP, ROW_HOP, FAR_HOP, RELAY_HOP, PERIOD = 15, 32, 36, 50, 27, 5
+CORE_HOP, CHIP_HOP, ROW_HOP, FAR_HOP, RELAY_HOP, PERIOD = 12, 28, 32, 60, 32, 5
 MESH = pl.DeviceIdType.MESH
 
 
 def kernel(
-    rows, cols, op_hbm, pos_ref, amp_ref, out_ref,
-    op_f32, hi_ref, lo_ref, hi_turned, lo_turned, pos_all, amp_all,
+    rows, cols, op_hbm, pos_hbm, amp_hbm, out_ref,
+    pos_ref, amp_ref, op_f32, hi_ref, lo_ref, hi_turned, lo_turned, pos_all, amp_all,
     north_in, west_in, south_in, east_in,
     south_out, east_out, north_out, west_out, passing,
-    op_sem, send_sem, recv_sem, pass_sem, onward_sem,
+    pos_sem, amp_sem, op_sem, send_sem, recv_sem, pass_sem, onward_sem,
 ):
     row = lax.axis_index("row")
     col = lax.axis_index("col")
@@ -26,7 +26,11 @@
     has_north, has_south = row > 0, row < rows - 1
     has_west, has_east = col > 0, col < cols - 1
 
+    load_pos = pltpu.make_async_copy(pos_hbm, pos_ref, pos_sem)
+    load_amp = pltpu.make_async_copy(amp_hbm, amp_ref, amp_sem)
     load = pltpu.make_async_copy(op_hbm.at[0, 0], op_f32, op_sem)
+    load_pos.start()
+    load_amp.start()
     load.start()
 
     middle, chip = rows // 2, cols // 4
@@ -65,6 +69,8 @@
             ref[...] = jnp.zeros_like(ref)
 
     shots = batches * batch
+    load_pos.wait()
+    load_amp.wait()
     pos_all[...] = jnp.transpose(jnp.broadcast_to(pos_ref[0], (128, shots)))
     amp_all[...] = jnp.transpose(jnp.broadcast_to(amp_ref[0], (128, shots)))
 
@@ -282,11 +288,13 @@
         out_shape=jax.ShapeDtypeStruct((1, 1, shots, order), jnp.float32),
         in_specs=[
             pl.BlockSpec(memory_space=pltpu.HBM),
-            pl.BlockSpec(memory_space=pltpu.VMEM),
-            pl.BlockSpec(memory_space=pltpu.VMEM),
+            pl.BlockSpec(memory_space=pltpu.HBM),
+            pl.BlockSpec(memory_space=pltpu.HBM),
         ],
         out_specs=pl.BlockSpec(memory_space=pltpu.VMEM),
         scratch_shapes=[
+            pltpu.VMEM((1, 1, shots), jnp.int32),
+            pltpu.VMEM((1, 1, shots), jnp.float32),
             pltpu.VMEM((order, order), jnp.float32),
             pltpu.VMEM((order, order), jnp.bfloat16),
             pltpu.VMEM((order, order), jnp.bfloat16),
@@ -297,13 +305,15 @@
             slots, slots, slots, slots,
             slots, slots, slots, slots, slots,
             pltpu.SemaphoreType.DMA,
+            pltpu.SemaphoreType.DMA,
+            pltpu.SemaphoreType.DMA,
             pltpu.SemaphoreType.DMA((4, batches)),
             pltpu.SemaphoreType.DMA((4, batches)),
             pltpu.SemaphoreType.DMA((batches,)),
             pltpu.SemaphoreType.DMA((batches,)),
         ],
         compiler_params=pltpu.CompilerParams(collective_id=0, has_side_effects=True, vmem_limit_bytes=52 << 20),
-    )(operators, positions, amplitudes)
+    )(*(pltpu.with_memory_space_constraint(x, pltpu.HBM) for x in (operators, positions, amplitudes)))
 
 
 def solution(mesh):

time: 47.1 us -> 45.5 us (0.966)
  local copies, waits for them, and re-layouts: 2.24 us -> 0.88 us
    unnamed x5 -> x1, local copies, waits for them, and re-layouts: 2.24 us -> 0.88 us
where the time goes in v3:
time: 45.5 us; the launch traced here: 45.3 us
  Pallas kernels  44.4 us (98%)
  local copies, waits for them, and re-layouts  0.88 us (2%)
    pallas_call x1, Pallas kernels, local(): pl.pallas_call(functools.partial(kernel, rows, cols), out_shape=jax.Shape...  44.4 us

profile of v3, /device:TPU:0, one launch (start us, length us, event | category | flops | bytes accessed | tf_op | source)
XLA Modules:
  0.0 45.3 jit_solution(17239347620182478891)
XLA Ops:
  0.0 44.4 %shard_map.37 = f32[1,1,256,768]{3,2,1,0:T(8,128)S(1)} custom-call(f32[1,1,768,768]{3,2,1,0:T(8,128)} %op_hbm.1, s32[1,1,256]{2,1,0:T(1,128)} %pos_hbm.1, f32[1,1,256]{2,1,0:T(1,128)} %amp_hbm.1), custom_call_target="tpu_custom_call" | custom-call | tf_op jit(solution)/shard_map/pallas_call | solution.py:286
  44.4 0.9 %copy.5 = f32[1,1,256,768]{3,2,1,0:T(8,128)} copy(f32[1,1,256,768]{3,2,1,0:T(8,128)S(1)} %shard_map.37) | data formatting | bytes 1572864

commit v4 on v3

--- a/solution.py
+++ b/solution.py
@@ -8,7 +8,8 @@
 from jax.sharding import PartitionSpec as P
 
 BATCH = 32
-CORE_HOP, CHIP_HOP, ROW_HOP, FAR_HOP, RELAY_HOP, PERIOD = 12, 28, 32, 60, 32, 5
+CORE_HOP, CHIP_HOP, ROW_HOP, FAR_HOP, RELAY_HOP, PERIOD = 15, 32, 36, 50, 27, 5
+DETOURS = 6
 MESH = pl.DeviceIdType.MESH
 
 
@@ -23,6 +24,7 @@
     col = lax.axis_index("col")
     batches, batch, half = north_in.shape
     order = 2 * half
+    detours = batches * DETOURS // 8
     has_north, has_south = row > 0, row < rows - 1
     has_west, has_east = col > 0, col < cols - 1
 
@@ -113,7 +115,7 @@
                 link(kind, b).start()
             return
 
-        around = jnp.logical_and(detour, (adj_zone if kind else fwd_zone))
+        around = jnp.logical_and(jnp.logical_and(detour, b < detours), (adj_zone if kind else fwd_zone))
 
         @pl.when(jnp.logical_and(present, jnp.logical_not(around)))
         def _():
@@ -226,7 +228,7 @@
         )
         now = jnp.where(fwd_next, lead_fwd + fwd * PERIOD, lead_adj + adj * PERIOD)
         pass_next = jnp.logical_and(
-            passed < batches,
+            passed < detours,
             jnp.logical_or(fwd + adj >= 2 * batches, lead_pass + passed * PERIOD <= now),
         )
         fwd_now = jnp.logical_and(fwd_next, jnp.logical_not(pass_next))
@@ -259,8 +261,8 @@
 
         return fwd + fwd_now.astype(jnp.int32), adj + adj_now.astype(jnp.int32), passed + pass_next.astype(jnp.int32)
 
-    start_pass = jnp.where(relays, 0, batches)
-    lax.fori_loop(0, 3 * batches - start_pass, tick, (jnp.int32(0), jnp.int32(0), start_pass))
+    start_pass = jnp.where(relays, 0, detours)
+    lax.fori_loop(0, 2 * batches + detours - start_pass, tick, (jnp.int32(0), jnp.int32(0), start_pass))
 
     def drain(b, carry):
         for kind, present in enumerate((has_south, has_east, has_north, has_west)):
@@ -268,7 +270,7 @@
             def _(kind=kind):
                 link(kind, b).wait_send()
 
-        @pl.when(relays)
+        @pl.when(jnp.logical_and(relays, b < detours))
         def _():
             onward(0, b).wait_send()
 

time: 45.5 us -> 45 us (0.989)
    pallas_call x1, Pallas kernels: 44.4 us -> 44 us  [local(): pl.pallas_call(functools.partial(kernel, rows, cols), out_shape=jax.Shape...]
where the time goes in v4:
time: 45 us; the launch traced here: 44.9 us
  Pallas kernels  44 us (98%)
  local copies, waits for them, and re-layouts  0.88 us (2%)
    pallas_call x1, Pallas kernels, local(): pl.pallas_call(functools.partial(kernel, rows, cols), out_shape=jax.Shape...  44 us

profile of v4, /device:TPU:0, one launch (start us, length us, event | category | flops | bytes accessed | tf_op | source)
XLA Modules:
  0.0 44.9 jit_solution(7693307369502958971)
XLA Ops:
  0.0 44.0 %shard_map.37 = f32[1,1,256,768]{3,2,1,0:T(8,128)S(1)} custom-call(f32[1,1,768,768]{3,2,1,0:T(8,128)} %op_hbm.1, s32[1,1,256]{2,1,0:T(1,128)} %pos_hbm.1, f32[1,1,256]{2,1,0:T(1,128)} %amp_hbm.1), custom_call_target="tpu_custom_call" | custom-call | tf_op jit(solution)/shard_map/pallas_call | solution.py:288
  44.0 0.9 %copy.5 = f32[1,1,256,768]{3,2,1,0:T(8,128)} copy(f32[1,1,256,768]{3,2,1,0:T(8,128)S(1)} %shard_map.37) | data formatting | bytes 1572864
